TPU v7x, 128 devices: a whole 4x4x4 slice. The times are simulated.
128 devices in a mesh: ctx: 8 (over y, z_hi), head: 4 (over z_lo, core), dp: 4 (over x).
Axes of the slice: x: 4, y: 4, z: 4 (z_hi: 2, z_lo: 2; z = z_hi * 2 + z_lo), core: 2. Of those that a mesh axis runs over, the one named last changes fastest.
Arguments:
- long_query: bfloat16 [24576, 8192], P(('dp', 'ctx', 'head')), parts along dimension 0, may hold values from -250 to 250
- long_kv: bfloat16 [2, 24576, 1024], P(None, ('dp', 'ctx', 'head')), parts along dimension 1, may hold values from -250 to 250
- short_query: bfloat16 [32768, 8192], P(('dp', 'ctx', 'head')), parts along dimension 0, may hold values from -250 to 250
- short_key_value: bfloat16 [2, 32768, 1024], P(None, ('dp', 'ctx', 'head')), parts along dimension 1, may hold values from -250 to 250
- short_seg: int32 [128, 256], P(('dp', 'ctx', 'head')), parts along dimension 0, may hold values from 0 to 7, never falling along the last dimension, each value on 1 to 128 neighbouring positions
Outputs:
- long_out: bfloat16 [24576, 8192], P(('dp', 'ctx', 'head')), parts along dimension 0
- short_out: bfloat16 [32768, 8192], P(('dp', 'ctx', 'head')), parts along dimension 0
There are 4 independent parts, one for each index of `dp`. A program takes and returns all parts, laid end to end along the dimension named above; each array names one. Nothing has to cross between parts.
All inputs are finite; a program needn't handle non-finite values.
Results may differ from a plain program's by a relative error of at most 0.0035.
Values may be sent and summed in bfloat16 or wider, within the bound.
A program may use at most 256 MiB of HBM per device.

v0:
```python
import math
import jax
import jax.numpy as jnp
from jax import lax
from jax.sharding import PartitionSpec as P

QUERY_HEAD_COUNT = 64
KEY_VALUE_HEADS = 8
HEAD_SIZE = 128
NEG_LARGE = -1e30


def blank_state(count_of_rows, kv_heads, head_groups):
    highest = jnp.full((kv_heads, head_groups, count_of_rows), NEG_LARGE, jnp.float32)
    totals = jnp.zeros((kv_heads, head_groups, count_of_rows), jnp.float32)
    accum = jnp.zeros((kv_heads, head_groups, count_of_rows, HEAD_SIZE), jnp.float32)
    return (highest, totals, accum)


def update_state(softmax_state, query_rows, stacked_rows, allowed):
    running_max, totals, accum = softmax_state
    kv_heads = query_rows.shape[1]
    head_dim = query_rows.shape[3]
    key_part = stacked_rows[0].reshape(stacked_rows.shape[1], kv_heads, head_dim)
    value_part = stacked_rows[1].reshape(stacked_rows.shape[1], kv_heads, head_dim)
    scores = jnp.einsum(
        "tkgd,skd->kgts", query_rows, key_part, preferred_element_type=jnp.float32
    ) * (1.0 / math.sqrt(head_dim))
    masked = jnp.where(allowed, scores, NEG_LARGE)
    new_max = jnp.maximum(running_max, jnp.max(masked, axis=-1))
    factor = jnp.exp(running_max - new_max)
    weights = jnp.where(allowed, jnp.exp(scores - new_max[..., None]), 0.0)
    totals = totals * factor + jnp.sum(weights, axis=-1)
    accum = accum * factor[..., None] + jnp.einsum(
        "kgts,skd->kgtd",
        weights.astype(jnp.bfloat16),
        value_part,
        preferred_element_type=jnp.float32,
    )
    return (new_max, totals, accum)


def finish_state(softmax_state):
    running_max, totals, accum = softmax_state
    mixed = (accum / totals[..., None]).astype(jnp.bfloat16)
    return mixed.transpose(2, 0, 1, 3).reshape(mixed.shape[2], -1)


def fold_long(query_rows, query_pos, block_length):

    def fold_step(running, shard_piece, begin_at):
        turns = shard_piece.shape[1] // block_length

        def one_turn(turn_index, inner_state):
            offset = begin_at + turn_index * block_length
            part_kv = lax.dynamic_slice_in_dim(
                shard_piece, turn_index * block_length, block_length, 1
            )
            key_pos = offset + jnp.arange(block_length, dtype=jnp.int32)
            allowed = key_pos[None, :] <= query_pos[:, None]
            return lax.cond(
                offset <= query_pos[-1],
                lambda held_state: update_state(held_state, query_rows, part_kv, allowed),
                lambda held_state: held_state,
                inner_state,
            )

        return lax.fori_loop(0, turns, one_turn, running)

    return fold_step


def attend_short(short_query, short_key_value, short_seg):
    sequence_length = short_query.shape[0]
    head_groups = QUERY_HEAD_COUNT // KEY_VALUE_HEADS
    query_rows = short_query.reshape(sequence_length, KEY_VALUE_HEADS, head_groups, HEAD_SIZE)
    labels = short_seg[0]
    positions = jnp.arange(sequence_length, dtype=jnp.int32)
    block_length = sequence_length // 4
    pieces_out = []
    for query_block in range(4):
        query_low = query_block * block_length
        query_high = query_low + block_length
        softmax_state = blank_state(block_length, KEY_VALUE_HEADS, head_groups)
        for key_block in range(query_block + 1):
            key_low = key_block * block_length
            key_high = key_low + block_length
            allowed = (
                positions[key_low:key_high][None, :] <= positions[query_low:query_high][:, None]
            ) & (labels[key_low:key_high][None, :] == labels[query_low:query_high][:, None])
            softmax_state = update_state(
                softmax_state,
                query_rows[query_low:query_high],
                short_key_value[:, key_low:key_high],
                allowed,
            )
        pieces_out.append(finish_state(softmax_state))
    return jnp.concatenate(pieces_out, axis=0)


def on_device(long_query, long_kv, short_query, short_key_value, short_seg):
    token_rows = long_query.shape[0]
    head_groups = QUERY_HEAD_COUNT // KEY_VALUE_HEADS
    window_count = lax.axis_size("ctx") * lax.axis_size("head")
    flat_rank = lax.axis_index("ctx") * lax.axis_size("head") + lax.axis_index("head")
    query_rows = long_query.reshape(token_rows, KEY_VALUE_HEADS, head_groups, HEAD_SIZE)
    query_pos = flat_rank * token_rows + jnp.arange(token_rows, dtype=jnp.int32)
    shards_per_block = 1
    while shards_per_block * token_rows < 512 and shards_per_block < window_count:
        shards_per_block = shards_per_block * 2
    gathered = lax.all_gather(long_kv, ("ctx", "head"), axis=1, tiled=True)
    fold_step = fold_long(query_rows, query_pos, shards_per_block * token_rows)
    softmax_state = fold_step(blank_state(token_rows, KEY_VALUE_HEADS, head_groups), gathered, 0)
    long_out = finish_state(softmax_state)
    short_out = attend_short(short_query, short_key_value, short_seg)
    return (long_out, short_out)


def solution(mesh):
    return jax.shard_map(
        on_device,
        mesh=mesh,
        in_specs=(
            P(("dp", "ctx", "head"), None),
            P(None, ("dp", "ctx", "head"), None),
            P(("dp", "ctx", "head"), None),
            P(None, ("dp", "ctx", "head"), None),
            P(("dp", "ctx", "head"), None),
        ),
        out_specs=(P(("dp", "ctx", "head"), None), P(("dp", "ctx", "head"), None)),
        check_vma=False,
    )
```

profile of v0, /device:TPU:89, one launch (start us, length us, event | category | flops | bytes accessed | tf_op | source)
XLA Modules:
  0.0 643.4 jit_solution(1320893152180307649)
XLA Ops:
  7.2 2.8 copy.69
  10.1 2.8 copy.193
  12.9 3.7 copy.71
  30.8 3.9 fusion.14
  48.9 3.0 fusion.31
  57.3 2.4 fusion.44
  61.1 1.9 fusion.53
  63.7 1.8 copy.320
  65.5 3.2 pad_maximum_fusion
  68.7 33.4 %all-gather.2.cloned.1.call-done = bf16[2,6144,1024]{2,0,1:T(2,128)(2,1)} async-done(((bf16[2,192,1024]{2,0,1:T(2,128)(2,1)}), bf16[2,6144,1024]{2,0,1:T(2,128)(2,1)}) %all-gather.2.cloned.1.call-update) | async-done | bytes 25165840 | tf_op jit(solution)/shard_map/all_gather | solution.py:111
  102.1 60.8 %copy.70 = bf16[2,6144,1024]{1,2,0:T(8,128)(2,1)} copy(bf16[2,6144,1024]{2,0,1:T(2,128)(2,1)} %all-gather.2.cloned.1.call-done) | data formatting | bytes 50331648 | tf_op jit(solution)/shard_map/while | solution.py:68
  162.9 3.4 broadcast_in_dim.168
  166.3 458.5 %while.17 = (s32[]{:T(128)}, f32[8,8,192]{2,1,0:T(8,128)S(1)}, f32[8,8,192]{2,1,0:T(8,128)S(1)}, f32[8,8,192,128]{3,2,1,0:T(8,128)}, s32[192]{0:T(256)S(1)}, /*i...) while((s32[]{:T(128)}, f32[8,8,192]{2,1,0:T(8,128)S(1)}, ...), condition=%wide.region_5.6_spmd, body=%wide.region_0.5_spmd.sunk | while | flops 4938966016 | bytes 190133392 | solution.py:68
  167.9 55.9 %conditional.2 = ((f32[8,8,192]{2,1,0:T(8,128)S(1)}, f32[8,8,192]{2,1,0:T(8,128)S(1)}, f32[8,8,192,128]{3,2,1,0:T(8,128)})) conditional(s32[]{:T(128)} %convert_element_type.108, (f32[8,8,192]{2,1,0:T(8,128)S(1)}, f32[8,8,192]{2,1,0:T(8,128)S(1)}, f32[8,8,192,128]{3,2,1,0:T(8,128)}) %tuple.107, (s32[]{:T(128)}, s32[1,768]{1,0:T(1,128)S(1)}, ...), branch_computations={%region_1.0_spmd, %region_2.4_spmd} | conditional | flops 4938966016 | bytes 190130080 | solution.py:61
  168.1 2.1 constant_dynamic-slice_fusion.1
  170.2 17.2 %fusion = (f32[8,8,192]{2,1,0:T(8,128)S(1)}, f32[8,768,192,8]{1,2,3,0:T(8,128)}) fusion(pred[192,768]{1,0:T(8,128)(4,1)S(1)} %broadcast_compare_fusion, bf16[768,8,128,1]{0,2,3,1:T(8,128)(2,1)S(1)} %bitcast.483, bf16[192,8,8,128]{3,0,2,1:T(8,128)(2,1)} %get-tuple-element.211), kind=kOutput, calls=%fused_computation.2 | convolution fusion | flops 2444218368 | bytes 42663936 | tf_op jit(solution)/shard_map/while/body/eval_jaxpr/cond/branch_1_fun/tkgd,skd->kgts/dot_general | solution.py:26
  187.4 17.0 %fusion.4 = f32[8,8,192]{2,1,0:T(8,128)S(1)} fusion(f32[8,768,192,8]{1,2,3,0:T(8,128)} %get-tuple-element.276, f32[8,8,192]{2,1,0:T(8,128)S(1)} %max.122, pred[192,768]{1,0:T(8,128)(4,1)S(1)} %broadcast_compare_fusion), kind=kLoop, calls=%fused_computation.6 | loop fusion | flops 37736448 | bytes 37994496 | tf_op jit(solution)/shard_map/while/body/eval_jaxpr/cond/branch_1_fun/reduce_sum | solution.py:33
  204.4 16.7 %multiply_add_fusion = f32[8,8,192,128]{3,2,1,0:T(8,128)S(1)} fusion(f32[8,8,192,128]{3,2,1,0:T(8,128)S(1)} %copy-done, f32[8,8,192]{2,1,0:T(8,128)S(1)} %get-tuple-element.260, bf16[768,8,128,1]{0,2,3,1:T(8,128)(2,1)S(1)} %bitcast.484, f32[8,768,192,8]{1,2,3,0:T(8,128)} %get-tuple-element.276, f32[8,8,192]{2,1,0:T(8,128)S(1)} %max.122, ...), kind=kOutput, calls=%fused_computation.9 | convolution fusion | flops 2456813568 | bytes 52150272 | tf_op jit(solution)/shard_map/while/body/eval_jaxpr/cond/branch_1_fun/kgts,skd->kgtd/dot_general | solution.py:34
  221.2 2.6 copy-done.1
  225.1 55.9 %conditional.2 = ((f32[8,8,192]{2,1,0:T(8,128)S(1)}, f32[8,8,192]{2,1,0:T(8,128)S(1)}, f32[8,8,192,128]{3,2,1,0:T(8,128)})) conditional(s32[]{:T(128)} %convert_element_type.108, (f32[8,8,192]{2,1,0:T(8,128)S(1)}, f32[8,8,192]{2,1,0:T(8,128)S(1)}, f32[8,8,192,128]{3,2,1,0:T(8,128)}) %tuple.107, (s32[]{:T(128)}, s32[1,768]{1,0:T(1,128)S(1)}, ...), branch_computations={%region_1.0_spmd, %region_2.4_spmd} | conditional | flops 4938966016 | bytes 190130080 | solution.py:61
  225.4 2.1 constant_dynamic-slice_fusion.1
  227.5 17.2 %fusion = (f32[8,8,192]{2,1,0:T(8,128)S(1)}, f32[8,768,192,8]{1,2,3,0:T(8,128)}) fusion(pred[192,768]{1,0:T(8,128)(4,1)S(1)} %broadcast_compare_fusion, bf16[768,8,128,1]{0,2,3,1:T(8,128)(2,1)S(1)} %bitcast.483, bf16[192,8,8,128]{3,0,2,1:T(8,128)(2,1)} %get-tuple-element.211), kind=kOutput, calls=%fused_computation.2 | convolution fusion | flops 2444218368 | bytes 42663936 | tf_op jit(solution)/shard_map/while/body/eval_jaxpr/cond/branch_1_fun/tkgd,skd->kgts/dot_general | solution.py:26
  244.6 17.0 %fusion.4 = f32[8,8,192]{2,1,0:T(8,128)S(1)} fusion(f32[8,768,192,8]{1,2,3,0:T(8,128)} %get-tuple-element.276, f32[8,8,192]{2,1,0:T(8,128)S(1)} %max.122, pred[192,768]{1,0:T(8,128)(4,1)S(1)} %broadcast_compare_fusion), kind=kLoop, calls=%fused_computation.6 | loop fusion | flops 37736448 | bytes 37994496 | tf_op jit(solution)/shard_map/while/body/eval_jaxpr/cond/branch_1_fun/reduce_sum | solution.py:33
  261.7 16.7 %multiply_add_fusion = f32[8,8,192,128]{3,2,1,0:T(8,128)S(1)} fusion(f32[8,8,192,128]{3,2,1,0:T(8,128)S(1)} %copy-done, f32[8,8,192]{2,1,0:T(8,128)S(1)} %get-tuple-element.260, bf16[768,8,128,1]{0,2,3,1:T(8,128)(2,1)S(1)} %bitcast.484, f32[8,768,192,8]{1,2,3,0:T(8,128)} %get-tuple-element.276, f32[8,8,192]{2,1,0:T(8,128)S(1)} %max.122, ...), kind=kOutput, calls=%fused_computation.9 | convolution fusion | flops 2456813568 | bytes 52150272 | tf_op jit(solution)/shard_map/while/body/eval_jaxpr/cond/branch_1_fun/kgts,skd->kgtd/dot_general | solution.py:34
  278.5 2.6 copy-done.1
  282.4 55.9 %conditional.2 = ((f32[8,8,192]{2,1,0:T(8,128)S(1)}, f32[8,8,192]{2,1,0:T(8,128)S(1)}, f32[8,8,192,128]{3,2,1,0:T(8,128)})) conditional(s32[]{:T(128)} %convert_element_type.108, (f32[8,8,192]{2,1,0:T(8,128)S(1)}, f32[8,8,192]{2,1,0:T(8,128)S(1)}, f32[8,8,192,128]{3,2,1,0:T(8,128)}) %tuple.107, (s32[]{:T(128)}, s32[1,768]{1,0:T(1,128)S(1)}, ...), branch_computations={%region_1.0_spmd, %region_2.4_spmd} | conditional | flops 4938966016 | bytes 190130080 | solution.py:61
  282.6 2.1 constant_dynamic-slice_fusion.1
  284.7 17.2 %fusion = (f32[8,8,192]{2,1,0:T(8,128)S(1)}, f32[8,768,192,8]{1,2,3,0:T(8,128)}) fusion(pred[192,768]{1,0:T(8,128)(4,1)S(1)} %broadcast_compare_fusion, bf16[768,8,128,1]{0,2,3,1:T(8,128)(2,1)S(1)} %bitcast.483, bf16[192,8,8,128]{3,0,2,1:T(8,128)(2,1)} %get-tuple-element.211), kind=kOutput, calls=%fused_computation.2 | convolution fusion | flops 2444218368 | bytes 42663936 | tf_op jit(solution)/shard_map/while/body/eval_jaxpr/cond/branch_1_fun/tkgd,skd->kgts/dot_general | solution.py:26
  301.9 17.0 %fusion.4 = f32[8,8,192]{2,1,0:T(8,128)S(1)} fusion(f32[8,768,192,8]{1,2,3,0:T(8,128)} %get-tuple-element.276, f32[8,8,192]{2,1,0:T(8,128)S(1)} %max.122, pred[192,768]{1,0:T(8,128)(4,1)S(1)} %broadcast_compare_fusion), kind=kLoop, calls=%fused_computation.6 | loop fusion | flops 37736448 | bytes 37994496 | tf_op jit(solution)/shard_map/while/body/eval_jaxpr/cond/branch_1_fun/reduce_sum | solution.py:33
  319.0 16.7 %multiply_add_fusion = f32[8,8,192,128]{3,2,1,0:T(8,128)S(1)} fusion(f32[8,8,192,128]{3,2,1,0:T(8,128)S(1)} %copy-done, f32[8,8,192]{2,1,0:T(8,128)S(1)} %get-tuple-element.260, bf16[768,8,128,1]{0,2,3,1:T(8,128)(2,1)S(1)} %bitcast.484, f32[8,768,192,8]{1,2,3,0:T(8,128)} %get-tuple-element.276, f32[8,8,192]{2,1,0:T(8,128)S(1)} %max.122, ...), kind=kOutput, calls=%fused_computation.9 | convolution fusion | flops 2456813568 | bytes 52150272 | tf_op jit(solution)/shard_map/while/body/eval_jaxpr/cond/branch_1_fun/kgts,skd->kgtd/dot_general | solution.py:34
  335.7 2.6 copy-done.1
  339.7 55.9 %conditional.2 = ((f32[8,8,192]{2,1,0:T(8,128)S(1)}, f32[8,8,192]{2,1,0:T(8,128)S(1)}, f32[8,8,192,128]{3,2,1,0:T(8,128)})) conditional(s32[]{:T(128)} %convert_element_type.108, (f32[8,8,192]{2,1,0:T(8,128)S(1)}, f32[8,8,192]{2,1,0:T(8,128)S(1)}, f32[8,8,192,128]{3,2,1,0:T(8,128)}) %tuple.107, (s32[]{:T(128)}, s32[1,768]{1,0:T(1,128)S(1)}, ...), branch_computations={%region_1.0_spmd, %region_2.4_spmd} | conditional | flops 4938966016 | bytes 190130080 | solution.py:61
  339.9 2.1 constant_dynamic-slice_fusion.1
  342.0 17.2 %fusion = (f32[8,8,192]{2,1,0:T(8,128)S(1)}, f32[8,768,192,8]{1,2,3,0:T(8,128)}) fusion(pred[192,768]{1,0:T(8,128)(4,1)S(1)} %broadcast_compare_fusion, bf16[768,8,128,1]{0,2,3,1:T(8,128)(2,1)S(1)} %bitcast.483, bf16[192,8,8,128]{3,0,2,1:T(8,128)(2,1)} %get-tuple-element.211), kind=kOutput, calls=%fused_computation.2 | convolution fusion | flops 2444218368 | bytes 42663936 | tf_op jit(solution)/shard_map/while/body/eval_jaxpr/cond/branch_1_fun/tkgd,skd->kgts/dot_general | solution.py:26
  359.2 17.0 %fusion.4 = f32[8,8,192]{2,1,0:T(8,128)S(1)} fusion(f32[8,768,192,8]{1,2,3,0:T(8,128)} %get-tuple-element.276, f32[8,8,192]{2,1,0:T(8,128)S(1)} %max.122, pred[192,768]{1,0:T(8,128)(4,1)S(1)} %broadcast_compare_fusion), kind=kLoop, calls=%fused_computation.6 | loop fusion | flops 37736448 | bytes 37994496 | tf_op jit(solution)/shard_map/while/body/eval_jaxpr/cond/branch_1_fun/reduce_sum | solution.py:33
  376.3 16.7 %multiply_add_fusion = f32[8,8,192,128]{3,2,1,0:T(8,128)S(1)} fusion(f32[8,8,192,128]{3,2,1,0:T(8,128)S(1)} %copy-done, f32[8,8,192]{2,1,0:T(8,128)S(1)} %get-tuple-element.260, bf16[768,8,128,1]{0,2,3,1:T(8,128)(2,1)S(1)} %bitcast.484, f32[8,768,192,8]{1,2,3,0:T(8,128)} %get-tuple-element.276, f32[8,8,192]{2,1,0:T(8,128)S(1)} %max.122, ...), kind=kOutput, calls=%fused_computation.9 | convolution fusion | flops 2456813568 | bytes 52150272 | tf_op jit(solution)/shard_map/while/body/eval_jaxpr/cond/branch_1_fun/kgts,skd->kgtd/dot_general | solution.py:34
  393.0 2.6 copy-done.1
  397.0 55.9 %conditional.2 = ((f32[8,8,192]{2,1,0:T(8,128)S(1)}, f32[8,8,192]{2,1,0:T(8,128)S(1)}, f32[8,8,192,128]{3,2,1,0:T(8,128)})) conditional(s32[]{:T(128)} %convert_element_type.108, (f32[8,8,192]{2,1,0:T(8,128)S(1)}, f32[8,8,192]{2,1,0:T(8,128)S(1)}, f32[8,8,192,128]{3,2,1,0:T(8,128)}) %tuple.107, (s32[]{:T(128)}, s32[1,768]{1,0:T(1,128)S(1)}, ...), branch_computations={%region_1.0_spmd, %region_2.4_spmd} | conditional | flops 4938966016 | bytes 190130080 | solution.py:61
  397.2 2.1 constant_dynamic-slice_fusion.1
  399.3 17.2 %fusion = (f32[8,8,192]{2,1,0:T(8,128)S(1)}, f32[8,768,192,8]{1,2,3,0:T(8,128)}) fusion(pred[192,768]{1,0:T(8,128)(4,1)S(1)} %broadcast_compare_fusion, bf16[768,8,128,1]{0,2,3,1:T(8,128)(2,1)S(1)} %bitcast.483, bf16[192,8,8,128]{3,0,2,1:T(8,128)(2,1)} %get-tuple-element.211), kind=kOutput, calls=%fused_computation.2 | convolution fusion | flops 2444218368 | bytes 42663936 | tf_op jit(solution)/shard_map/while/body/eval_jaxpr/cond/branch_1_fun/tkgd,skd->kgts/dot_general | solution.py:26
  416.5 17.0 %fusion.4 = f32[8,8,192]{2,1,0:T(8,128)S(1)} fusion(f32[8,768,192,8]{1,2,3,0:T(8,128)} %get-tuple-element.276, f32[8,8,192]{2,1,0:T(8,128)S(1)} %max.122, pred[192,768]{1,0:T(8,128)(4,1)S(1)} %broadcast_compare_fusion), kind=kLoop, calls=%fused_computation.6 | loop fusion | flops 37736448 | bytes 37994496 | tf_op jit(solution)/shard_map/while/body/eval_jaxpr/cond/branch_1_fun/reduce_sum | solution.py:33
  433.6 16.7 %multiply_add_fusion = f32[8,8,192,128]{3,2,1,0:T(8,128)S(1)} fusion(f32[8,8,192,128]{3,2,1,0:T(8,128)S(1)} %copy-done, f32[8,8,192]{2,1,0:T(8,128)S(1)} %get-tuple-element.260, bf16[768,8,128,1]{0,2,3,1:T(8,128)(2,1)S(1)} %bitcast.484, f32[8,768,192,8]{1,2,3,0:T(8,128)} %get-tuple-element.276, f32[8,8,192]{2,1,0:T(8,128)S(1)} %max.122, ...), kind=kOutput, calls=%fused_computation.9 | convolution fusion | flops 2456813568 | bytes 52150272 | tf_op jit(solution)/shard_map/while/body/eval_jaxpr/cond/branch_1_fun/kgts,skd->kgtd/dot_general | solution.py:34
  450.3 2.6 copy-done.1
  454.3 55.9 %conditional.2 = ((f32[8,8,192]{2,1,0:T(8,128)S(1)}, f32[8,8,192]{2,1,0:T(8,128)S(1)}, f32[8,8,192,128]{3,2,1,0:T(8,128)})) conditional(s32[]{:T(128)} %convert_element_type.108, (f32[8,8,192]{2,1,0:T(8,128)S(1)}, f32[8,8,192]{2,1,0:T(8,128)S(1)}, f32[8,8,192,128]{3,2,1,0:T(8,128)}) %tuple.107, (s32[]{:T(128)}, s32[1,768]{1,0:T(1,128)S(1)}, ...), branch_computations={%region_1.0_spmd, %region_2.4_spmd} | conditional | flops 4938966016 | bytes 190130080 | solution.py:61
  454.5 2.1 constant_dynamic-slice_fusion.1
  456.6 17.2 %fusion = (f32[8,8,192]{2,1,0:T(8,128)S(1)}, f32[8,768,192,8]{1,2,3,0:T(8,128)}) fusion(pred[192,768]{1,0:T(8,128)(4,1)S(1)} %broadcast_compare_fusion, bf16[768,8,128,1]{0,2,3,1:T(8,128)(2,1)S(1)} %bitcast.483, bf16[192,8,8,128]{3,0,2,1:T(8,128)(2,1)} %get-tuple-element.211), kind=kOutput, calls=%fused_computation.2 | convolution fusion | flops 2444218368 | bytes 42663936 | tf_op jit(solution)/shard_map/while/body/eval_jaxpr/cond/branch_1_fun/tkgd,skd->kgts/dot_general | solution.py:26
  473.8 17.0 %fusion.4 = f32[8,8,192]{2,1,0:T(8,128)S(1)} fusion(f32[8,768,192,8]{1,2,3,0:T(8,128)} %get-tuple-element.276, f32[8,8,192]{2,1,0:T(8,128)S(1)} %max.122, pred[192,768]{1,0:T(8,128)(4,1)S(1)} %broadcast_compare_fusion), kind=kLoop, calls=%fused_computation.6 | loop fusion | flops 37736448 | bytes 37994496 | tf_op jit(solution)/shard_map/while/body/eval_jaxpr/cond/branch_1_fun/reduce_sum | solution.py:33
  490.8 16.7 %multiply_add_fusion = f32[8,8,192,128]{3,2,1,0:T(8,128)S(1)} fusion(f32[8,8,192,128]{3,2,1,0:T(8,128)S(1)} %copy-done, f32[8,8,192]{2,1,0:T(8,128)S(1)} %get-tuple-element.260, bf16[768,8,128,1]{0,2,3,1:T(8,128)(2,1)S(1)} %bitcast.484, f32[8,768,192,8]{1,2,3,0:T(8,128)} %get-tuple-element.276, f32[8,8,192]{2,1,0:T(8,128)S(1)} %max.122, ...), kind=kOutput, calls=%fused_computation.9 | convolution fusion | flops 2456813568 | bytes 52150272 | tf_op jit(solution)/shard_map/while/body/eval_jaxpr/cond/branch_1_fun/kgts,skd->kgtd/dot_general | solution.py:34
  507.6 2.6 copy-done.1
  511.6 55.9 %conditional.2 = ((f32[8,8,192]{2,1,0:T(8,128)S(1)}, f32[8,8,192]{2,1,0:T(8,128)S(1)}, f32[8,8,192,128]{3,2,1,0:T(8,128)})) conditional(s32[]{:T(128)} %convert_element_type.108, (f32[8,8,192]{2,1,0:T(8,128)S(1)}, f32[8,8,192]{2,1,0:T(8,128)S(1)}, f32[8,8,192,128]{3,2,1,0:T(8,128)}) %tuple.107, (s32[]{:T(128)}, s32[1,768]{1,0:T(1,128)S(1)}, ...), branch_computations={%region_1.0_spmd, %region_2.4_spmd} | conditional | flops 4938966016 | bytes 190130080 | solution.py:61
  511.8 2.1 constant_dynamic-slice_fusion.1
  513.9 17.2 %fusion = (f32[8,8,192]{2,1,0:T(8,128)S(1)}, f32[8,768,192,8]{1,2,3,0:T(8,128)}) fusion(pred[192,768]{1,0:T(8,128)(4,1)S(1)} %broadcast_compare_fusion, bf16[768,8,128,1]{0,2,3,1:T(8,128)(2,1)S(1)} %bitcast.483, bf16[192,8,8,128]{3,0,2,1:T(8,128)(2,1)} %get-tuple-element.211), kind=kOutput, calls=%fused_computation.2 | convolution fusion | flops 2444218368 | bytes 42663936 | tf_op jit(solution)/shard_map/while/body/eval_jaxpr/cond/branch_1_fun/tkgd,skd->kgts/dot_general | solution.py:26
  531.0 17.0 %fusion.4 = f32[8,8,192]{2,1,0:T(8,128)S(1)} fusion(f32[8,768,192,8]{1,2,3,0:T(8,128)} %get-tuple-element.276, f32[8,8,192]{2,1,0:T(8,128)S(1)} %max.122, pred[192,768]{1,0:T(8,128)(4,1)S(1)} %broadcast_compare_fusion), kind=kLoop, calls=%fused_computation.6 | loop fusion | flops 37736448 | bytes 37994496 | tf_op jit(solution)/shard_map/while/body/eval_jaxpr/cond/branch_1_fun/reduce_sum | solution.py:33
  548.1 16.7 %multiply_add_fusion = f32[8,8,192,128]{3,2,1,0:T(8,128)S(1)} fusion(f32[8,8,192,128]{3,2,1,0:T(8,128)S(1)} %copy-done, f32[8,8,192]{2,1,0:T(8,128)S(1)} %get-tuple-element.260, bf16[768,8,128,1]{0,2,3,1:T(8,128)(2,1)S(1)} %bitcast.484, f32[8,768,192,8]{1,2,3,0:T(8,128)} %get-tuple-element.276, f32[8,8,192]{2,1,0:T(8,128)S(1)} %max.122, ...), kind=kOutput, calls=%fused_computation.9 | convolution fusion | flops 2456813568 | bytes 52150272 | tf_op jit(solution)/shard_map/while/body/eval_jaxpr/cond/branch_1_fun/kgts,skd->kgtd/dot_general | solution.py:34
  564.9 2.6 copy-done.1
  568.8 56.0 %conditional.2 = ((f32[8,8,192]{2,1,0:T(8,128)S(1)}, f32[8,8,192]{2,1,0:T(8,128)S(1)}, f32[8,8,192,128]{3,2,1,0:T(8,128)})) conditional(s32[]{:T(128)} %convert_element_type.108, (f32[8,8,192]{2,1,0:T(8,128)S(1)}, f32[8,8,192]{2,1,0:T(8,128)S(1)}, f32[8,8,192,128]{3,2,1,0:T(8,128)}) %tuple.107, (s32[]{:T(128)}, s32[1,768]{1,0:T(1,128)S(1)}, ...), branch_computations={%region_1.0_spmd, %region_2.4_spmd} | conditional | flops 4938966016 | bytes 190130080 | solution.py:61
  569.0 2.2 constant_dynamic-slice_fusion.1
  571.2 17.2 %fusion = (f32[8,8,192]{2,1,0:T(8,128)S(1)}, f32[8,768,192,8]{1,2,3,0:T(8,128)}) fusion(pred[192,768]{1,0:T(8,128)(4,1)S(1)} %broadcast_compare_fusion, bf16[768,8,128,1]{0,2,3,1:T(8,128)(2,1)S(1)} %bitcast.483, bf16[192,8,8,128]{3,0,2,1:T(8,128)(2,1)} %get-tuple-element.211), kind=kOutput, calls=%fused_computation.2 | convolution fusion | flops 2444218368 | bytes 42663936 | tf_op jit(solution)/shard_map/while/body/eval_jaxpr/cond/branch_1_fun/tkgd,skd->kgts/dot_general | solution.py:26
  588.4 17.0 %fusion.4 = f32[8,8,192]{2,1,0:T(8,128)S(1)} fusion(f32[8,768,192,8]{1,2,3,0:T(8,128)} %get-tuple-element.276, f32[8,8,192]{2,1,0:T(8,128)S(1)} %max.122, pred[192,768]{1,0:T(8,128)(4,1)S(1)} %broadcast_compare_fusion), kind=kLoop, calls=%fused_computation.6 | loop fusion | flops 37736448 | bytes 37994496 | tf_op jit(solution)/shard_map/while/body/eval_jaxpr/cond/branch_1_fun/reduce_sum | solution.py:33
  605.5 16.7 %multiply_add_fusion = f32[8,8,192,128]{3,2,1,0:T(8,128)S(1)} fusion(f32[8,8,192,128]{3,2,1,0:T(8,128)S(1)} %copy-done, f32[8,8,192]{2,1,0:T(8,128)S(1)} %get-tuple-element.260, bf16[768,8,128,1]{0,2,3,1:T(8,128)(2,1)S(1)} %bitcast.484, f32[8,768,192,8]{1,2,3,0:T(8,128)} %get-tuple-element.276, f32[8,8,192]{2,1,0:T(8,128)S(1)} %max.122, ...), kind=kOutput, calls=%fused_computation.9 | convolution fusion | flops 2456813568 | bytes 52150272 | tf_op jit(solution)/shard_map/while/body/eval_jaxpr/cond/branch_1_fun/kgts,skd->kgtd/dot_general | solution.py:34
  622.2 2.6 copy-done.1
  624.8 4.7 fusion.12
  629.5 2.0 copy.72
  631.6 4.5 copy.316
  (154 shorter events, 42.8 us)
Async XLA Ops:
  7.2 95.0 %all-gather.2.cloned.1.call-start = ((), (), s32[]{:S(2)}) async-start(), calls=%async_computation | async-start | bytes 25952256 | tf_op jit(solution)/shard_map/all_gather | solution.py:111
  12.8 3.9 copy-start.2
  16.6 0.6 copy-start.5
  17.1 1.2 copy-start.3
  18.3 0.7 copy-start.4
  18.4 0.8 slice-start
  187.3 17.1 %copy-start = (f32[8,8,192,128]{3,2,1,0:T(8,128)S(1)}, f32[8,8,192,128]{3,2,1,0:T(8,128)}, u32[]{:S(2)}) copy-start(f32[8,8,192,128]{3,2,1,0:T(8,128)} %get-tuple-element.213) | copy-start | bytes 18874372 | tf_op jit(solution)/shard_map/while/body/eval_jaxpr/cond
  221.2 2.6 copy-start.1
  244.6 17.1 %copy-start = (f32[8,8,192,128]{3,2,1,0:T(8,128)S(1)}, f32[8,8,192,128]{3,2,1,0:T(8,128)}, u32[]{:S(2)}) copy-start(f32[8,8,192,128]{3,2,1,0:T(8,128)} %get-tuple-element.213) | copy-start | bytes 18874372 | tf_op jit(solution)/shard_map/while/body/eval_jaxpr/cond
  278.4 2.6 copy-start.1
  301.9 17.1 %copy-start = (f32[8,8,192,128]{3,2,1,0:T(8,128)S(1)}, f32[8,8,192,128]{3,2,1,0:T(8,128)}, u32[]{:S(2)}) copy-start(f32[8,8,192,128]{3,2,1,0:T(8,128)} %get-tuple-element.213) | copy-start | bytes 18874372 | tf_op jit(solution)/shard_map/while/body/eval_jaxpr/cond
  335.7 2.6 copy-start.1
  359.2 17.1 %copy-start = (f32[8,8,192,128]{3,2,1,0:T(8,128)S(1)}, f32[8,8,192,128]{3,2,1,0:T(8,128)}, u32[]{:S(2)}) copy-start(f32[8,8,192,128]{3,2,1,0:T(8,128)} %get-tuple-element.213) | copy-start | bytes 18874372 | tf_op jit(solution)/shard_map/while/body/eval_jaxpr/cond
  393.0 2.6 copy-start.1
  416.5 17.1 %copy-start = (f32[8,8,192,128]{3,2,1,0:T(8,128)S(1)}, f32[8,8,192,128]{3,2,1,0:T(8,128)}, u32[]{:S(2)}) copy-start(f32[8,8,192,128]{3,2,1,0:T(8,128)} %get-tuple-element.213) | copy-start | bytes 18874372 | tf_op jit(solution)/shard_map/while/body/eval_jaxpr/cond
  450.3 2.6 copy-start.1
  473.7 17.1 %copy-start = (f32[8,8,192,128]{3,2,1,0:T(8,128)S(1)}, f32[8,8,192,128]{3,2,1,0:T(8,128)}, u32[]{:S(2)}) copy-start(f32[8,8,192,128]{3,2,1,0:T(8,128)} %get-tuple-element.213) | copy-start | bytes 18874372 | tf_op jit(solution)/shard_map/while/body/eval_jaxpr/cond
  507.6 2.6 copy-start.1
  531.0 17.1 %copy-start = (f32[8,8,192,128]{3,2,1,0:T(8,128)S(1)}, f32[8,8,192,128]{3,2,1,0:T(8,128)}, u32[]{:S(2)}) copy-start(f32[8,8,192,128]{3,2,1,0:T(8,128)} %get-tuple-element.213) | copy-start | bytes 18874372 | tf_op jit(solution)/shard_map/while/body/eval_jaxpr/cond
  564.9 2.6 copy-start.1
  588.4 17.1 %copy-start = (f32[8,8,192,128]{3,2,1,0:T(8,128)S(1)}, f32[8,8,192,128]{3,2,1,0:T(8,128)}, u32[]{:S(2)}) copy-start(f32[8,8,192,128]{3,2,1,0:T(8,128)} %get-tuple-element.213) | copy-start | bytes 18874372 | tf_op jit(solution)/shard_map/while/body/eval_jaxpr/cond
  622.2 2.6 copy-start.1
Sparse Core Ops, SparseCore 0:
  10.2 91.8 all-gather.1
where the time goes:
time: 656 us; the launch traced here: 643 us
  matrix products  302 us (46%)
  other arithmetic  153 us (23%)
  local copies, waits for them, and re-layouts  133 us (20%)
  waiting for transfers between devices  33.4 us (5%)
  between operations  14.9 us (2%)
  loops' own time  6.58 us (1%)
    dot_general x18, matrix products, update_state(): jnp.einsum('tkgd,skd->kgts', query_rows, key_part, preferred_element_type...  153 us
    dot_general x18, matrix products, update_state(): jnp.einsum('kgts,skd->kgtd', weights.astype(jnp.bfloat16), value_part, pr...  149 us
    reduce_sum x13, other arithmetic, update_state(): totals = totals * factor + jnp.sum(weights, axis=-1)  143 us
    while x2, local copies, waits for them, and re-layouts, fold_step(): return lax.fori_loop(0, turns, one_turn, running)  64.4 us
    all_gather x1, waiting for transfers between devices, on_device(): gathered = lax.all_gather(long_kv, ('ctx', 'head'), axis=1, tiled=True)  33.4 us
    cond x40, local copies, waits for them, and re-layouts  21 us
    unnamed x29, local copies, waits for them, and re-layouts  17 us
    slice x8, local copies, waits for them, and re-layouts, update_state(): stacked_rows[1].reshape(stacked_rows.shape[1], kv_heads, head_dim)  16.9 us
  transfers between devices with their start and end apart: 1, of which 1 were waited for; matrix products, arithmetic and copies ran while one was open for 9% of the time, Pallas kernels for 0%

commit v1 on v0

--- a/solution.py
+++ b/solution.py
@@ -108,7 +108,12 @@
     shards_per_block = 1
     while shards_per_block * token_rows < 512 and shards_per_block < window_count:
         shards_per_block = shards_per_block * 2
-    gathered = lax.all_gather(long_kv, ("ctx", "head"), axis=1, tiled=True)
+    gathered = jnp.concatenate(
+        lax.all_to_all(
+            jnp.stack([long_kv] * lax.axis_size(("ctx", "head"))), ("ctx", "head"), 0, 0
+        ),
+        axis=1,
+    )
     fold_step = fold_long(query_rows, query_pos, shards_per_block * token_rows)
     softmax_state = fold_step(blank_state(token_rows, KEY_VALUE_HEADS, head_groups), gathered, 0)
     long_out = finish_state(softmax_state)

time: 656 us -> 901 us (1.37)
  the two profiles are of different devices: /device:TPU:89 before, /device:TPU:125 now
where the time goes in v1:
time: 901 us; the launch traced here: 889 us
  matrix products  302 us (34%)
  waiting for transfers between devices  287 us (32%)
  other arithmetic  153 us (17%)
  local copies, waits for them, and re-layouts  131 us (15%)
    all_to_all x1, waiting for transfers between devices, on_device(): lax.all_to_all(jnp.stack([long_kv] * lax.axis_size(('ctx', 'head'))), ('c...  287 us
    dot_general x18, matrix products, update_state(): jnp.einsum('tkgd,skd->kgts', query_rows, key_part, preferred_element_type...  153 us
    dot_general x18, matrix products, update_state(): jnp.einsum('kgts,skd->kgtd', weights.astype(jnp.bfloat16), value_part, pr...  149 us
    reduce_sum x13, other arithmetic, update_state(): totals = totals * factor + jnp.sum(weights, axis=-1)  143 us
    while x2, local copies, waits for them, and re-layouts, fold_step(): return lax.fori_loop(0, turns, one_turn, running)  36.4 us
    cond x40, local copies, waits for them, and re-layouts  21.3 us
    all_to_all x1, local copies, waits for them, and re-layouts, on_device(): lax.all_to_all(jnp.stack([long_kv] * lax.axis_size(('ctx', 'head'))), ('c...  21 us
  transfers between devices with their start and end apart: 1, of which 1 were waited for; matrix products, arithmetic and copies ran while one was open for 6% of the time, Pallas kernels for 0%

profile of v1, /device:TPU:125, one launch (start us, length us, event | category | flops | bytes accessed | tf_op | source)
XLA Modules:
  0.0 888.8 jit_solution(9188883630036323506)
XLA Ops:
  0.6 9.5 %stack.2 = bf16[32,2,192,1024]{3,2,1,0:T(8,128)(2,1)} broadcast(bf16[2,192,1024]{2,1,0:T(8,128)(2,1)} %param.10), dimensions={1,2,3} | broadcast | bytes 25952256 | tf_op jit(solution)/shard_map/stack | solution.py:113
  10.1 7.6 all-to-all-start
  18.7 3.7 copy.120
  36.7 3.9 fusion.14
  54.8 3.0 fusion.31
  63.1 2.4 fusion.44
  67.0 1.9 fusion.53
  71.3 3.2 pad_maximum_fusion
  74.5 287.0 %all-to-all-done = bf16[32,2,192,1024]{3,2,1,0:T(8,128)(2,1)} async-done(((bf16[32,2,192,1024]{3,2,1,0:T(8,128)(2,1)}), bf16[32,2,192,1024]{3,2,1,0:T(8,128)(2,1)}, u32[]{:S(2)}, u32[]{:S(2)}) %all-to-all-start) | async-done | bytes 25165856 | tf_op jit(solution)/shard_map/all_to_all | solution.py:112
  361.4 21.0 %copy.118 = bf16[32,2,192,1024]{3,2,0,1:T(8,128)(2,1)} copy(bf16[32,2,192,1024]{3,2,1,0:T(8,128)(2,1)} %all-to-all-done) | data formatting | bytes 50331648 | tf_op jit(solution)/shard_map/all_to_all | solution.py:112
  382.4 32.8 %copy.119 = bf16[2,6144,1024]{1,2,0:T(8,128)(2,1)} copy(bf16[2,6144,1024]{2,1,0:T(8,128)(2,1)} %bitcast.487) | data formatting | bytes 50331648 | tf_op jit(solution)/shard_map/while | solution.py:68
  415.2 3.4 broadcast_in_dim.168
  418.6 458.5 %while.17 = (s32[]{:T(128)}, f32[8,8,192]{2,1,0:T(8,128)S(1)}, f32[8,8,192]{2,1,0:T(8,128)S(1)}, f32[8,8,192,128]{3,2,1,0:T(8,128)}, s32[192]{0:T(256)S(1)}, /*i...) while((s32[]{:T(128)}, f32[8,8,192]{2,1,0:T(8,128)S(1)}, ...), condition=%wide.region_5.6_spmd, body=%wide.region_0.5_spmd.sunk | while | flops 4938966016 | bytes 190133392 | solution.py:68
  420.2 55.9 %conditional.2 = ((f32[8,8,192]{2,1,0:T(8,128)S(1)}, f32[8,8,192]{2,1,0:T(8,128)S(1)}, f32[8,8,192,128]{3,2,1,0:T(8,128)})) conditional(s32[]{:T(128)} %convert_element_type.108, (f32[8,8,192]{2,1,0:T(8,128)S(1)}, f32[8,8,192]{2,1,0:T(8,128)S(1)}, f32[8,8,192,128]{3,2,1,0:T(8,128)}) %tuple.108, (s32[]{:T(128)}, s32[1,768]{1,0:T(1,128)S(1)}, ...), branch_computations={%region_1.0_spmd, %region_2.4_spmd} | conditional | flops 4938966016 | bytes 190130080 | solution.py:61
  420.4 2.1 constant_dynamic-slice_fusion.1
  422.5 17.1 %fusion = (f32[8,8,192]{2,1,0:T(8,128)S(1)}, f32[8,768,192,8]{1,2,3,0:T(8,128)}) fusion(pred[192,768]{1,0:T(8,128)(4,1)S(1)} %broadcast_compare_fusion, bf16[768,8,128,1]{0,2,3,1:T(8,128)(2,1)S(1)} %bitcast.486, bf16[192,8,8,128]{3,0,2,1:T(8,128)(2,1)} %get-tuple-element.211), kind=kOutput, calls=%fused_computation.2 | convolution fusion | flops 2444218368 | bytes 42663936 | tf_op jit(solution)/shard_map/while/body/eval_jaxpr/cond/branch_1_fun/tkgd,skd->kgts/dot_general | solution.py:26
  439.6 17.0 %fusion.4 = f32[8,8,192]{2,1,0:T(8,128)S(1)} fusion(f32[8,768,192,8]{1,2,3,0:T(8,128)} %get-tuple-element.283, f32[8,8,192]{2,1,0:T(8,128)S(1)} %max.122, pred[192,768]{1,0:T(8,128)(4,1)S(1)} %broadcast_compare_fusion), kind=kLoop, calls=%fused_computation.6 | loop fusion | flops 37736448 | bytes 37994496 | tf_op jit(solution)/shard_map/while/body/eval_jaxpr/cond/branch_1_fun/reduce_sum | solution.py:33
  456.7 16.7 %multiply_add_fusion = f32[8,8,192,128]{3,2,1,0:T(8,128)S(1)} fusion(f32[8,8,192,128]{3,2,1,0:T(8,128)S(1)} %copy-done, f32[8,8,192]{2,1,0:T(8,128)S(1)} %get-tuple-element.267, bf16[768,8,128,1]{0,2,3,1:T(8,128)(2,1)S(1)} %bitcast.488, f32[8,768,192,8]{1,2,3,0:T(8,128)} %get-tuple-element.283, f32[8,8,192]{2,1,0:T(8,128)S(1)} %max.122, ...), kind=kOutput, calls=%fused_computation.9 | convolution fusion | flops 2456813568 | bytes 52150272 | tf_op jit(solution)/shard_map/while/body/eval_jaxpr/cond/branch_1_fun/kgts,skd->kgtd/dot_general | solution.py:34
  473.4 2.6 copy-done.1
  477.5 55.9 %conditional.2 = ((f32[8,8,192]{2,1,0:T(8,128)S(1)}, f32[8,8,192]{2,1,0:T(8,128)S(1)}, f32[8,8,192,128]{3,2,1,0:T(8,128)})) conditional(s32[]{:T(128)} %convert_element_type.108, (f32[8,8,192]{2,1,0:T(8,128)S(1)}, f32[8,8,192]{2,1,0:T(8,128)S(1)}, f32[8,8,192,128]{3,2,1,0:T(8,128)}) %tuple.108, (s32[]{:T(128)}, s32[1,768]{1,0:T(1,128)S(1)}, ...), branch_computations={%region_1.0_spmd, %region_2.4_spmd} | conditional | flops 4938966016 | bytes 190130080 | solution.py:61
  477.7 2.1 constant_dynamic-slice_fusion.1
  479.8 17.1 %fusion = (f32[8,8,192]{2,1,0:T(8,128)S(1)}, f32[8,768,192,8]{1,2,3,0:T(8,128)}) fusion(pred[192,768]{1,0:T(8,128)(4,1)S(1)} %broadcast_compare_fusion, bf16[768,8,128,1]{0,2,3,1:T(8,128)(2,1)S(1)} %bitcast.486, bf16[192,8,8,128]{3,0,2,1:T(8,128)(2,1)} %get-tuple-element.211), kind=kOutput, calls=%fused_computation.2 | convolution fusion | flops 2444218368 | bytes 42663936 | tf_op jit(solution)/shard_map/while/body/eval_jaxpr/cond/branch_1_fun/tkgd,skd->kgts/dot_general | solution.py:26
  496.9 17.0 %fusion.4 = f32[8,8,192]{2,1,0:T(8,128)S(1)} fusion(f32[8,768,192,8]{1,2,3,0:T(8,128)} %get-tuple-element.283, f32[8,8,192]{2,1,0:T(8,128)S(1)} %max.122, pred[192,768]{1,0:T(8,128)(4,1)S(1)} %broadcast_compare_fusion), kind=kLoop, calls=%fused_computation.6 | loop fusion | flops 37736448 | bytes 37994496 | tf_op jit(solution)/shard_map/while/body/eval_jaxpr/cond/branch_1_fun/reduce_sum | solution.py:33
  514.0 16.7 %multiply_add_fusion = f32[8,8,192,128]{3,2,1,0:T(8,128)S(1)} fusion(f32[8,8,192,128]{3,2,1,0:T(8,128)S(1)} %copy-done, f32[8,8,192]{2,1,0:T(8,128)S(1)} %get-tuple-element.267, bf16[768,8,128,1]{0,2,3,1:T(8,128)(2,1)S(1)} %bitcast.488, f32[8,768,192,8]{1,2,3,0:T(8,128)} %get-tuple-element.283, f32[8,8,192]{2,1,0:T(8,128)S(1)} %max.122, ...), kind=kOutput, calls=%fused_computation.9 | convolution fusion | flops 2456813568 | bytes 52150272 | tf_op jit(solution)/shard_map/while/body/eval_jaxpr/cond/branch_1_fun/kgts,skd->kgtd/dot_general | solution.py:34
  530.7 2.6 copy-done.1
  534.7 55.9 %conditional.2 = ((f32[8,8,192]{2,1,0:T(8,128)S(1)}, f32[8,8,192]{2,1,0:T(8,128)S(1)}, f32[8,8,192,128]{3,2,1,0:T(8,128)})) conditional(s32[]{:T(128)} %convert_element_type.108, (f32[8,8,192]{2,1,0:T(8,128)S(1)}, f32[8,8,192]{2,1,0:T(8,128)S(1)}, f32[8,8,192,128]{3,2,1,0:T(8,128)}) %tuple.108, (s32[]{:T(128)}, s32[1,768]{1,0:T(1,128)S(1)}, ...), branch_computations={%region_1.0_spmd, %region_2.4_spmd} | conditional | flops 4938966016 | bytes 190130080 | solution.py:61
  534.9 2.1 constant_dynamic-slice_fusion.1
  537.1 17.1 %fusion = (f32[8,8,192]{2,1,0:T(8,128)S(1)}, f32[8,768,192,8]{1,2,3,0:T(8,128)}) fusion(pred[192,768]{1,0:T(8,128)(4,1)S(1)} %broadcast_compare_fusion, bf16[768,8,128,1]{0,2,3,1:T(8,128)(2,1)S(1)} %bitcast.486, bf16[192,8,8,128]{3,0,2,1:T(8,128)(2,1)} %get-tuple-element.211), kind=kOutput, calls=%fused_computation.2 | convolution fusion | flops 2444218368 | bytes 42663936 | tf_op jit(solution)/shard_map/while/body/eval_jaxpr/cond/branch_1_fun/tkgd,skd->kgts/dot_general | solution.py:26
  554.2 17.0 %fusion.4 = f32[8,8,192]{2,1,0:T(8,128)S(1)} fusion(f32[8,768,192,8]{1,2,3,0:T(8,128)} %get-tuple-element.283, f32[8,8,192]{2,1,0:T(8,128)S(1)} %max.122, pred[192,768]{1,0:T(8,128)(4,1)S(1)} %broadcast_compare_fusion), kind=kLoop, calls=%fused_computation.6 | loop fusion | flops 37736448 | bytes 37994496 | tf_op jit(solution)/shard_map/while/body/eval_jaxpr/cond/branch_1_fun/reduce_sum | solution.py:33
  571.3 16.7 %multiply_add_fusion = f32[8,8,192,128]{3,2,1,0:T(8,128)S(1)} fusion(f32[8,8,192,128]{3,2,1,0:T(8,128)S(1)} %copy-done, f32[8,8,192]{2,1,0:T(8,128)S(1)} %get-tuple-element.267, bf16[768,8,128,1]{0,2,3,1:T(8,128)(2,1)S(1)} %bitcast.488, f32[8,768,192,8]{1,2,3,0:T(8,128)} %get-tuple-element.283, f32[8,8,192]{2,1,0:T(8,128)S(1)} %max.122, ...), kind=kOutput, calls=%fused_computation.9 | convolution fusion | flops 2456813568 | bytes 52150272 | tf_op jit(solution)/shard_map/while/body/eval_jaxpr/cond/branch_1_fun/kgts,skd->kgtd/dot_general | solution.py:34
  588.0 2.6 copy-done.1
  592.0 55.9 %conditional.2 = ((f32[8,8,192]{2,1,0:T(8,128)S(1)}, f32[8,8,192]{2,1,0:T(8,128)S(1)}, f32[8,8,192,128]{3,2,1,0:T(8,128)})) conditional(s32[]{:T(128)} %convert_element_type.108, (f32[8,8,192]{2,1,0:T(8,128)S(1)}, f32[8,8,192]{2,1,0:T(8,128)S(1)}, f32[8,8,192,128]{3,2,1,0:T(8,128)}) %tuple.108, (s32[]{:T(128)}, s32[1,768]{1,0:T(1,128)S(1)}, ...), branch_computations={%region_1.0_spmd, %region_2.4_spmd} | conditional | flops 4938966016 | bytes 190130080 | solution.py:61
  592.2 2.1 constant_dynamic-slice_fusion.1
  594.3 17.1 %fusion = (f32[8,8,192]{2,1,0:T(8,128)S(1)}, f32[8,768,192,8]{1,2,3,0:T(8,128)}) fusion(pred[192,768]{1,0:T(8,128)(4,1)S(1)} %broadcast_compare_fusion, bf16[768,8,128,1]{0,2,3,1:T(8,128)(2,1)S(1)} %bitcast.486, bf16[192,8,8,128]{3,0,2,1:T(8,128)(2,1)} %get-tuple-element.211), kind=kOutput, calls=%fused_computation.2 | convolution fusion | flops 2444218368 | bytes 42663936 | tf_op jit(solution)/shard_map/while/body/eval_jaxpr/cond/branch_1_fun/tkgd,skd->kgts/dot_general | solution.py:26
  611.5 17.0 %fusion.4 = f32[8,8,192]{2,1,0:T(8,128)S(1)} fusion(f32[8,768,192,8]{1,2,3,0:T(8,128)} %get-tuple-element.283, f32[8,8,192]{2,1,0:T(8,128)S(1)} %max.122, pred[192,768]{1,0:T(8,128)(4,1)S(1)} %broadcast_compare_fusion), kind=kLoop, calls=%fused_computation.6 | loop fusion | flops 37736448 | bytes 37994496 | tf_op jit(solution)/shard_map/while/body/eval_jaxpr/cond/branch_1_fun/reduce_sum | solution.py:33
  628.6 16.7 %multiply_add_fusion = f32[8,8,192,128]{3,2,1,0:T(8,128)S(1)} fusion(f32[8,8,192,128]{3,2,1,0:T(8,128)S(1)} %copy-done, f32[8,8,192]{2,1,0:T(8,128)S(1)} %get-tuple-element.267, bf16[768,8,128,1]{0,2,3,1:T(8,128)(2,1)S(1)} %bitcast.488, f32[8,768,192,8]{1,2,3,0:T(8,128)} %get-tuple-element.283, f32[8,8,192]{2,1,0:T(8,128)S(1)} %max.122, ...), kind=kOutput, calls=%fused_computation.9 | convolution fusion | flops 2456813568 | bytes 52150272 | tf_op jit(solution)/shard_map/while/body/eval_jaxpr/cond/branch_1_fun/kgts,skd->kgtd/dot_general | solution.py:34
  645.3 2.6 copy-done.1
  649.3 55.9 %conditional.2 = ((f32[8,8,192]{2,1,0:T(8,128)S(1)}, f32[8,8,192]{2,1,0:T(8,128)S(1)}, f32[8,8,192,128]{3,2,1,0:T(8,128)})) conditional(s32[]{:T(128)} %convert_element_type.108, (f32[8,8,192]{2,1,0:T(8,128)S(1)}, f32[8,8,192]{2,1,0:T(8,128)S(1)}, f32[8,8,192,128]{3,2,1,0:T(8,128)}) %tuple.108, (s32[]{:T(128)}, s32[1,768]{1,0:T(1,128)S(1)}, ...), branch_computations={%region_1.0_spmd, %region_2.4_spmd} | conditional | flops 4938966016 | bytes 190130080 | solution.py:61
  649.5 2.1 constant_dynamic-slice_fusion.1
  651.6 17.1 %fusion = (f32[8,8,192]{2,1,0:T(8,128)S(1)}, f32[8,768,192,8]{1,2,3,0:T(8,128)}) fusion(pred[192,768]{1,0:T(8,128)(4,1)S(1)} %broadcast_compare_fusion, bf16[768,8,128,1]{0,2,3,1:T(8,128)(2,1)S(1)} %bitcast.486, bf16[192,8,8,128]{3,0,2,1:T(8,128)(2,1)} %get-tuple-element.211), kind=kOutput, calls=%fused_computation.2 | convolution fusion | flops 2444218368 | bytes 42663936 | tf_op jit(solution)/shard_map/while/body/eval_jaxpr/cond/branch_1_fun/tkgd,skd->kgts/dot_general | solution.py:26
  668.8 17.0 %fusion.4 = f32[8,8,192]{2,1,0:T(8,128)S(1)} fusion(f32[8,768,192,8]{1,2,3,0:T(8,128)} %get-tuple-element.283, f32[8,8,192]{2,1,0:T(8,128)S(1)} %max.122, pred[192,768]{1,0:T(8,128)(4,1)S(1)} %broadcast_compare_fusion), kind=kLoop, calls=%fused_computation.6 | loop fusion | flops 37736448 | bytes 37994496 | tf_op jit(solution)/shard_map/while/body/eval_jaxpr/cond/branch_1_fun/reduce_sum | solution.py:33
  685.9 16.7 %multiply_add_fusion = f32[8,8,192,128]{3,2,1,0:T(8,128)S(1)} fusion(f32[8,8,192,128]{3,2,1,0:T(8,128)S(1)} %copy-done, f32[8,8,192]{2,1,0:T(8,128)S(1)} %get-tuple-element.267, bf16[768,8,128,1]{0,2,3,1:T(8,128)(2,1)S(1)} %bitcast.488, f32[8,768,192,8]{1,2,3,0:T(8,128)} %get-tuple-element.283, f32[8,8,192]{2,1,0:T(8,128)S(1)} %max.122, ...), kind=kOutput, calls=%fused_computation.9 | convolution fusion | flops 2456813568 | bytes 52150272 | tf_op jit(solution)/shard_map/while/body/eval_jaxpr/cond/branch_1_fun/kgts,skd->kgtd/dot_general | solution.py:34
  702.6 2.6 copy-done.1
  706.6 55.9 %conditional.2 = ((f32[8,8,192]{2,1,0:T(8,128)S(1)}, f32[8,8,192]{2,1,0:T(8,128)S(1)}, f32[8,8,192,128]{3,2,1,0:T(8,128)})) conditional(s32[]{:T(128)} %convert_element_type.108, (f32[8,8,192]{2,1,0:T(8,128)S(1)}, f32[8,8,192]{2,1,0:T(8,128)S(1)}, f32[8,8,192,128]{3,2,1,0:T(8,128)}) %tuple.108, (s32[]{:T(128)}, s32[1,768]{1,0:T(1,128)S(1)}, ...), branch_computations={%region_1.0_spmd, %region_2.4_spmd} | conditional | flops 4938966016 | bytes 190130080 | solution.py:61
  706.8 2.1 constant_dynamic-slice_fusion.1
  708.9 17.1 %fusion = (f32[8,8,192]{2,1,0:T(8,128)S(1)}, f32[8,768,192,8]{1,2,3,0:T(8,128)}) fusion(pred[192,768]{1,0:T(8,128)(4,1)S(1)} %broadcast_compare_fusion, bf16[768,8,128,1]{0,2,3,1:T(8,128)(2,1)S(1)} %bitcast.486, bf16[192,8,8,128]{3,0,2,1:T(8,128)(2,1)} %get-tuple-element.211), kind=kOutput, calls=%fused_computation.2 | convolution fusion | flops 2444218368 | bytes 42663936 | tf_op jit(solution)/shard_map/while/body/eval_jaxpr/cond/branch_1_fun/tkgd,skd->kgts/dot_general | solution.py:26
  726.1 17.0 %fusion.4 = f32[8,8,192]{2,1,0:T(8,128)S(1)} fusion(f32[8,768,192,8]{1,2,3,0:T(8,128)} %get-tuple-element.283, f32[8,8,192]{2,1,0:T(8,128)S(1)} %max.122, pred[192,768]{1,0:T(8,128)(4,1)S(1)} %broadcast_compare_fusion), kind=kLoop, calls=%fused_computation.6 | loop fusion | flops 37736448 | bytes 37994496 | tf_op jit(solution)/shard_map/while/body/eval_jaxpr/cond/branch_1_fun/reduce_sum | solution.py:33
  743.1 16.7 %multiply_add_fusion = f32[8,8,192,128]{3,2,1,0:T(8,128)S(1)} fusion(f32[8,8,192,128]{3,2,1,0:T(8,128)S(1)} %copy-done, f32[8,8,192]{2,1,0:T(8,128)S(1)} %get-tuple-element.267, bf16[768,8,128,1]{0,2,3,1:T(8,128)(2,1)S(1)} %bitcast.488, f32[8,768,192,8]{1,2,3,0:T(8,128)} %get-tuple-element.283, f32[8,8,192]{2,1,0:T(8,128)S(1)} %max.122, ...), kind=kOutput, calls=%fused_computation.9 | convolution fusion | flops 2456813568 | bytes 52150272 | tf_op jit(solution)/shard_map/while/body/eval_jaxpr/cond/branch_1_fun/kgts,skd->kgtd/dot_general | solution.py:34
  759.9 2.6 copy-done.1
  763.9 55.9 %conditional.2 = ((f32[8,8,192]{2,1,0:T(8,128)S(1)}, f32[8,8,192]{2,1,0:T(8,128)S(1)}, f32[8,8,192,128]{3,2,1,0:T(8,128)})) conditional(s32[]{:T(128)} %convert_element_type.108, (f32[8,8,192]{2,1,0:T(8,128)S(1)}, f32[8,8,192]{2,1,0:T(8,128)S(1)}, f32[8,8,192,128]{3,2,1,0:T(8,128)}) %tuple.108, (s32[]{:T(128)}, s32[1,768]{1,0:T(1,128)S(1)}, ...), branch_computations={%region_1.0_spmd, %region_2.4_spmd} | conditional | flops 4938966016 | bytes 190130080 | solution.py:61
  764.1 2.1 constant_dynamic-slice_fusion.1
  766.2 17.1 %fusion = (f32[8,8,192]{2,1,0:T(8,128)S(1)}, f32[8,768,192,8]{1,2,3,0:T(8,128)}) fusion(pred[192,768]{1,0:T(8,128)(4,1)S(1)} %broadcast_compare_fusion, bf16[768,8,128,1]{0,2,3,1:T(8,128)(2,1)S(1)} %bitcast.486, bf16[192,8,8,128]{3,0,2,1:T(8,128)(2,1)} %get-tuple-element.211), kind=kOutput, calls=%fused_computation.2 | convolution fusion | flops 2444218368 | bytes 42663936 | tf_op jit(solution)/shard_map/while/body/eval_jaxpr/cond/branch_1_fun/tkgd,skd->kgts/dot_general | solution.py:26
  783.4 17.0 %fusion.4 = f32[8,8,192]{2,1,0:T(8,128)S(1)} fusion(f32[8,768,192,8]{1,2,3,0:T(8,128)} %get-tuple-element.283, f32[8,8,192]{2,1,0:T(8,128)S(1)} %max.122, pred[192,768]{1,0:T(8,128)(4,1)S(1)} %broadcast_compare_fusion), kind=kLoop, calls=%fused_computation.6 | loop fusion | flops 37736448 | bytes 37994496 | tf_op jit(solution)/shard_map/while/body/eval_jaxpr/cond/branch_1_fun/reduce_sum | solution.py:33
  800.4 16.7 %multiply_add_fusion = f32[8,8,192,128]{3,2,1,0:T(8,128)S(1)} fusion(f32[8,8,192,128]{3,2,1,0:T(8,128)S(1)} %copy-done, f32[8,8,192]{2,1,0:T(8,128)S(1)} %get-tuple-element.267, bf16[768,8,128,1]{0,2,3,1:T(8,128)(2,1)S(1)} %bitcast.488, f32[8,768,192,8]{1,2,3,0:T(8,128)} %get-tuple-element.283, f32[8,8,192]{2,1,0:T(8,128)S(1)} %max.122, ...), kind=kOutput, calls=%fused_computation.9 | convolution fusion | flops 2456813568 | bytes 52150272 | tf_op jit(solution)/shard_map/while/body/eval_jaxpr/cond/branch_1_fun/kgts,skd->kgtd/dot_general | solution.py:34
  817.2 2.6 copy-done.1
  821.2 55.9 %conditional.2 = ((f32[8,8,192]{2,1,0:T(8,128)S(1)}, f32[8,8,192]{2,1,0:T(8,128)S(1)}, f32[8,8,192,128]{3,2,1,0:T(8,128)})) conditional(s32[]{:T(128)} %convert_element_type.108, (f32[8,8,192]{2,1,0:T(8,128)S(1)}, f32[8,8,192]{2,1,0:T(8,128)S(1)}, f32[8,8,192,128]{3,2,1,0:T(8,128)}) %tuple.108, (s32[]{:T(128)}, s32[1,768]{1,0:T(1,128)S(1)}, ...), branch_computations={%region_1.0_spmd, %region_2.4_spmd} | conditional | flops 4938966016 | bytes 190130080 | solution.py:61
  821.4 2.1 constant_dynamic-slice_fusion.1
  823.5 17.1 %fusion = (f32[8,8,192]{2,1,0:T(8,128)S(1)}, f32[8,768,192,8]{1,2,3,0:T(8,128)}) fusion(pred[192,768]{1,0:T(8,128)(4,1)S(1)} %broadcast_compare_fusion, bf16[768,8,128,1]{0,2,3,1:T(8,128)(2,1)S(1)} %bitcast.486, bf16[192,8,8,128]{3,0,2,1:T(8,128)(2,1)} %get-tuple-element.211), kind=kOutput, calls=%fused_computation.2 | convolution fusion | flops 2444218368 | bytes 42663936 | tf_op jit(solution)/shard_map/while/body/eval_jaxpr/cond/branch_1_fun/tkgd,skd->kgts/dot_general | solution.py:26
  840.6 17.0 %fusion.4 = f32[8,8,192]{2,1,0:T(8,128)S(1)} fusion(f32[8,768,192,8]{1,2,3,0:T(8,128)} %get-tuple-element.283, f32[8,8,192]{2,1,0:T(8,128)S(1)} %max.122, pred[192,768]{1,0:T(8,128)(4,1)S(1)} %broadcast_compare_fusion), kind=kLoop, calls=%fused_computation.6 | loop fusion | flops 37736448 | bytes 37994496 | tf_op jit(solution)/shard_map/while/body/eval_jaxpr/cond/branch_1_fun/reduce_sum | solution.py:33
  857.7 16.7 %multiply_add_fusion = f32[8,8,192,128]{3,2,1,0:T(8,128)S(1)} fusion(f32[8,8,192,128]{3,2,1,0:T(8,128)S(1)} %copy-done, f32[8,8,192]{2,1,0:T(8,128)S(1)} %get-tuple-element.267, bf16[768,8,128,1]{0,2,3,1:T(8,128)(2,1)S(1)} %bitcast.488, f32[8,768,192,8]{1,2,3,0:T(8,128)} %get-tuple-element.283, f32[8,8,192]{2,1,0:T(8,128)S(1)} %max.122, ...), kind=kOutput, calls=%fused_computation.9 | convolution fusion | flops 2456813568 | bytes 52150272 | tf_op jit(solution)/shard_map/while/body/eval_jaxpr/cond/branch_1_fun/kgts,skd->kgtd/dot_general | solution.py:34
  874.5 2.6 copy-done.1
  877.1 4.7 fusion.12
  881.8 2.0 copy.121
  883.9 4.5 copy.365
  (156 shorter events, 45.3 us)
Async XLA Ops:
  10.1 7.7 copy-start.3
  10.1 351.3 %all-to-all-start = ((bf16[32,2,192,1024]{3,2,1,0:T(8,128)(2,1)}), bf16[32,2,192,1024]{3,2,1,0:T(8,128)(2,1)}, u32[]{:S(2)}, u32[]{:S(2)}) async-start(bf16[32,2,192,1024]{3,2,1,0:T(8,128)(2,1)} %stack.2), calls=%async_computation | async-start | bytes 50331648 | tf_op jit(solution)/shard_map/all_to_all | solution.py:112
  18.7 3.9 copy-start.2
  22.4 0.6 copy-start.6
  23.0 1.2 copy-start.4
  24.2 0.7 copy-start.5
  24.2 0.8 slice-start
  439.6 17.1 %copy-start = (f32[8,8,192,128]{3,2,1,0:T(8,128)S(1)}, f32[8,8,192,128]{3,2,1,0:T(8,128)}, u32[]{:S(2)}) copy-start(f32[8,8,192,128]{3,2,1,0:T(8,128)} %get-tuple-element.213) | copy-start | bytes 18874372 | tf_op jit(solution)/shard_map/while/body/eval_jaxpr/cond
  473.4 2.7 copy-start.1
  496.9 17.1 %copy-start = (f32[8,8,192,128]{3,2,1,0:T(8,128)S(1)}, f32[8,8,192,128]{3,2,1,0:T(8,128)}, u32[]{:S(2)}) copy-start(f32[8,8,192,128]{3,2,1,0:T(8,128)} %get-tuple-element.213) | copy-start | bytes 18874372 | tf_op jit(solution)/shard_map/while/body/eval_jaxpr/cond
  530.7 2.7 copy-start.1
  554.2 17.1 %copy-start = (f32[8,8,192,128]{3,2,1,0:T(8,128)S(1)}, f32[8,8,192,128]{3,2,1,0:T(8,128)}, u32[]{:S(2)}) copy-start(f32[8,8,192,128]{3,2,1,0:T(8,128)} %get-tuple-element.213) | copy-start | bytes 18874372 | tf_op jit(solution)/shard_map/while/body/eval_jaxpr/cond
  588.0 2.7 copy-start.1
  611.5 17.1 %copy-start = (f32[8,8,192,128]{3,2,1,0:T(8,128)S(1)}, f32[8,8,192,128]{3,2,1,0:T(8,128)}, u32[]{:S(2)}) copy-start(f32[8,8,192,128]{3,2,1,0:T(8,128)} %get-tuple-element.213) | copy-start | bytes 18874372 | tf_op jit(solution)/shard_map/while/body/eval_jaxpr/cond
  645.3 2.7 copy-start.1
  668.8 17.1 %copy-start = (f32[8,8,192,128]{3,2,1,0:T(8,128)S(1)}, f32[8,8,192,128]{3,2,1,0:T(8,128)}, u32[]{:S(2)}) copy-start(f32[8,8,192,128]{3,2,1,0:T(8,128)} %get-tuple-element.213) | copy-start | bytes 18874372 | tf_op jit(solution)/shard_map/while/body/eval_jaxpr/cond
  702.6 2.7 copy-start.1
  726.0 17.1 %copy-start = (f32[8,8,192,128]{3,2,1,0:T(8,128)S(1)}, f32[8,8,192,128]{3,2,1,0:T(8,128)}, u32[]{:S(2)}) copy-start(f32[8,8,192,128]{3,2,1,0:T(8,128)} %get-tuple-element.213) | copy-start | bytes 18874372 | tf_op jit(solution)/shard_map/while/body/eval_jaxpr/cond
  759.9 2.7 copy-start.1
  783.3 17.1 %copy-start = (f32[8,8,192,128]{3,2,1,0:T(8,128)S(1)}, f32[8,8,192,128]{3,2,1,0:T(8,128)}, u32[]{:S(2)}) copy-start(f32[8,8,192,128]{3,2,1,0:T(8,128)} %get-tuple-element.213) | copy-start | bytes 18874372 | tf_op jit(solution)/shard_map/while/body/eval_jaxpr/cond
  817.2 2.7 copy-start.1
  840.6 17.1 %copy-start = (f32[8,8,192,128]{3,2,1,0:T(8,128)S(1)}, f32[8,8,192,128]{3,2,1,0:T(8,128)}, u32[]{:S(2)}) copy-start(f32[8,8,192,128]{3,2,1,0:T(8,128)} %get-tuple-element.213) | copy-start | bytes 18874372 | tf_op jit(solution)/shard_map/while/body/eval_jaxpr/cond
  874.4 2.7 copy-start.1
